TPU v7x, 32 devices: a whole 2x2x4 slice. The times are simulated.
32 devices in a mesh: stn: 4 (over z), chan: 8 (over y, x, core).
Axes of the slice: x: 2, y: 2, z: 4, core: 2. Of those that a mesh axis runs over, the one named last changes fastest.
Arguments:
- voltages: bfloat16 [1024, 8, 8, 1024], P('stn', 'chan'), may hold values from -6 to 6
- fir_taps: float32 [8, 8, 1024], replicated, may hold values from -2.5 to 2.5
Outputs:
- visibilities: float32 [4, 64, 2, 1024, 1024], P(None, 'chan', None, 'stn')
All inputs are finite; a program needn't handle non-finite values.
Results may differ from a plain program's by a relative error of at most 0.0044.
Values may be sent and summed in bfloat16 or wider, within the bound.
No kernel may reach another device: no remote copies, remote signals or barrier semaphores. Data moves between devices by JAX's collectives and lax.ppermute only.
A program may use at most 192 MiB of HBM per device.

v0:
```python
import math
import jax
import jax.numpy as jnp
from jax import lax
from jax.sharding import PartitionSpec as P

AVG = 16


def shifted(block, axis, distance):
    devices = range(lax.axis_size(axis))
    route = [(i - distance, i) for i in devices if i - distance in devices]
    return lax.ppermute(block, axis, route)


def rotation(numbers, modulus):
    angles = (numbers % modulus).astype(jnp.float32) * jnp.float32(-2.0 * math.pi / modulus)
    return (jnp.cos(angles), jnp.sin(angles))


def split_pair(table):
    upper = table.astype(jnp.bfloat16)
    lower = (table - upper.astype(jnp.float32)).astype(jnp.bfloat16)
    return (upper, lower)


def complex_table(real_part, imag_part, axis_at):
    first = jnp.stack([real_part, imag_part], axis=-1)
    second = jnp.stack([-imag_part, real_part], axis=-1)
    return jnp.stack([first, second], axis=axis_at)


def per_device(voltages, fir_taps):
    inputs_dev, _, frames_dev, slot_count = voltages.shape
    phases = fir_taps.shape[0]
    tap_count = fir_taps.shape[1]
    lane_count = lax.axis_size("chan")
    groups = lane_count // phases
    position = lax.axis_index("chan")
    my_phase = position % phases
    my_group = position // phases
    recent = voltages[:, 0]
    if groups > 1:
        earlier = shifted(voltages[:, 0, frames_dev - (tap_count - 1) :, :], "chan", phases)
    else:
        earlier = jnp.zeros((inputs_dev, tap_count - 1, slot_count), voltages.dtype)
    series = jnp.concatenate([earlier, recent], axis=1)
    coeffs = lax.dynamic_index_in_dim(fir_taps, my_phase, 0, keepdims=False)
    frame_ids = my_group * frames_dev + jnp.arange(frames_dev, dtype=jnp.int32)
    keep_mask = (frame_ids >= tap_count - 1).astype(jnp.float32)
    filtered = sum(
        (
            coeffs[tap_index]
            * series[:, tap_count - 1 - tap_index : tap_count - 1 - tap_index + frames_dev].astype(
                jnp.float32
            )
            for tap_index in range(tap_count)
        )
    )
    filtered = filtered * keep_mask[None, :, None]
    better = lax.Precision.HIGH
    split_len = slot_count // phases
    folded = filtered.reshape(inputs_dev, frames_dev, split_len, phases)
    slot_ids = jnp.arange(split_len, dtype=jnp.int32)
    short_re, short_im = rotation(slot_ids[:, None] * slot_ids[None, :], split_len)
    short_table = jnp.stack([short_re, short_im], axis=-1)
    inner = jnp.einsum(
        "ifqr,qvc->rvcfi", folded, short_table, precision=better, preferred_element_type=jnp.float32
    )
    rest_ids = jnp.arange(phases, dtype=jnp.int32)
    freq_ids = jnp.arange(slot_count, dtype=jnp.int32).reshape(phases, split_len)
    twist_re, twist_im = rotation(
        (my_phase + phases * rest_ids)[:, None, None] * freq_ids[None], phases * slot_count
    )
    twist_table = complex_table(twist_re, twist_im, 3)
    branch = jnp.einsum(
        "rvcfi,ruvcd->uvfdi",
        inner,
        twist_table,
        precision=better,
        preferred_element_type=jnp.float32,
    )
    branch = branch.reshape(slot_count, 1, frames_dev, 2, inputs_dev).astype(jnp.bfloat16)
    band_count = phases // 2
    band_re, band_im = rotation(
        rest_ids[:, None] * jnp.arange(band_count, dtype=jnp.int32)[None, :], phases
    )
    band_table = complex_table(band_re, band_im, 1)
    band_upper, band_lower = split_pair(band_table)
    turned = lax.all_to_all(branch, "chan", split_axis=0, concat_axis=1, tiled=True)
    span_len = turned.shape[0]
    sources = turned.shape[1]
    item_count = turned.shape[2]
    grouped = turned.reshape(span_len, sources // phases, phases, item_count, 2, inputs_dev)
    phase_form = "wgpfci,pcbd->bwgfdi"
    total = jnp.einsum(
        phase_form, grouped, band_upper, preferred_element_type=jnp.float32
    ) + jnp.einsum(phase_form, grouped, band_lower, preferred_element_type=jnp.float32)
    spectra = total.astype(jnp.bfloat16)
    span_dev = spectra.shape[1]
    subs_dev = span_dev // AVG
    stacked = spectra.reshape(band_count, subs_dev, AVG * groups * frames_dev, 2, inputs_dev)
    columns = stacked.reshape(band_count, subs_dev, -1, inputs_dev)
    swapped = jnp.stack([stacked[:, :, :, 1], -stacked[:, :, :, 0]], axis=3).reshape(
        band_count, subs_dev, -1, inputs_dev
    )
    left_side = jnp.stack([columns, swapped], axis=2)
    spectra_count = groups * frames_dev - (tap_count - 1)
    scaling = 1.0 / (phases * slot_count * AVG * spectra_count)
    vis_form = "bsokn,bskw->bsonw"
    return (
        jnp.einsum(
            vis_form,
            left_side,
            lax.all_gather(columns, "stn", axis=3, tiled=True),
            preferred_element_type=jnp.float32,
        )
        * scaling
    )


def solution(mesh):
    return jax.shard_map(
        per_device,
        mesh=mesh,
        in_specs=(P("stn", "chan", None, None), P()),
        out_specs=P(None, "chan", None, "stn", None),
        check_vma=False,
    )
```

profile of v0, /device:TPU:0, one launch (start us, length us, event | category | flops | bytes accessed | tf_op | source)
XLA Modules:
  0.0 559.5 jit_solution(15071491346341078132)
XLA Ops:
  6.5 0.3 fusion.36
  6.9 0.2 fusion.38
  7.1 0.5 copy.40
  7.6 0.5 copy.41
  8.1 6.9 %copy.42 = bf16[256,1,8,1024]{0,3,2,1:T(8,128)(2,1)} copy(bf16[256,1,8,1024]{3,2,1,0:T(8,128)(2,1)} %param.2) | data formatting | bytes 8388608 | tf_op args[0]
  15.0 1.1 constant_dynamic-slice_fusion.6
  16.1 12.6 %multiply_bitcast_fusion = f32[256,8,128,8]{0,3,2,1:T(8,128)} fusion(bf16[256,8,1024]{0,2,1:T(8,128)(2,1)} %bitcast.96, f32[8]{0:T(128)S(1)} %compare_convert_fusion, f32[1024]{0:T(1024)S(1)} %bitcast.107, f32[1024]{0:T(1024)S(1)} %bitcast.101, f32[1024]{0:T(1024)S(1)} %bitcast.102, f32[1024]{0:T(1024)S(1)} %bitcast.103, f32[1024]{0:T(1024)S(1)} %bitcast.104, ...), kind=kLoop, calls=%fused_computation.24 | loop fusion | flops 50331648 | bytes 12615712 | tf_op jit(solution)/shard_map/reshape | solution.py:63
  28.7 9.1 %copy.44 = f32[256,8,128,8]{2,0,3,1:T(8,128)} copy(f32[256,8,128,8]{0,3,2,1:T(8,128)} %multiply_bitcast_fusion) | data formatting | bytes 16777216 | tf_op jit(solution)/shard_map/reshape | solution.py:63
  37.8 14.2 %fusion.18 = f32[8,128,2,8,256,1]{4,1,0,3,2,5:T(8,128)} fusion(f32[256,8,128,8]{2,0,3,1:T(8,128)} %copy.44, f32[128,128,1]{1,0,2:T(8,128)S(1)} %get-tuple-element.24, f32[128,128,1]{1,0,2:T(8,128)S(1)} %get-tuple-element.25), kind=kOutput, calls=%fused_computation.27 | convolution fusion | flops 3221258240 | bytes 25296896 | tf_op jit(solution)/shard_map/ifqr,qvc->rvcfi/dot_general | solution.py:67
  52.0 25.0 %fusion.3 = bf16[8,128,8,2,256]{4,0,2,3,1:T(8,128)(2,1)} fusion(f32[8,128,2,8,256,1]{4,1,0,3,2,5:T(8,128)} %fusion.18, f32[8,8,128,1,2]{0,1,3,4,2:T(8,128)S(1)} %bitcast.99, f32[8,8,128,1,2]{0,1,3,4,2:T(8,128)S(1)} %bitcast.98), kind=kOutput, calls=%fused_computation.12 | convolution fusion | flops 406880256 | bytes 25296896 | tf_op jit(solution)/shard_map/rvcfi,ruvcd->uvfdi/dot_general | solution.py:76
  77.0 8.5 %copy.46 = bf16[8,128,8,2,256]{4,2,3,1,0:T(8,128)(2,1)} copy(bf16[8,128,8,2,256]{4,0,2,3,1:T(8,128)(2,1)} %fusion.3) | data formatting | bytes 16777216 | tf_op jit(solution)/shard_map/convert_element_type | solution.py:83
  85.5 16.0 %all-to-all-start = ((bf16[1024,1,8,2,256]{4,2,3,1,0:T(8,128)(2,1)}), bf16[1024,1,8,2,256]{4,2,3,1,0:T(8,128)(2,1)}, u32[]{:S(2)}, u32[]{:S(2)}) async-start(bf16[1024,1,8,2,256]{4,2,3,1,0:T(8,128)(2,1)} %bitcast.95), calls=%async_computation | async-start | bytes 16777216 | tf_op jit(solution)/shard_map/all_to_all | solution.py:90
  101.5 0.0 all-gather.2.cloned.1.call-start
  101.6 0.1 fusion.52
  101.6 0.1 fusion.50
  101.7 94.6 %all-to-all-done = bf16[1024,1,8,2,256]{4,2,3,1,0:T(8,128)(2,1)} async-done(((bf16[1024,1,8,2,256]{4,2,3,1,0:T(8,128)(2,1)}), bf16[1024,1,8,2,256]{4,2,3,1,0:T(8,128)(2,1)}, u32[]{:S(2)}, u32[]{:S(2)}) %all-to-all-start) | async-done | bytes 8388640 | tf_op jit(solution)/shard_map/all_to_all | solution.py:90
  196.3 12.6 %fusion.8 = f32[4,2,128,8,256,1]{4,0,5,3,2,1:T(4,128)} fusion(bf16[8,128,1,8,2,256]{5,3,4,2,1,0:T(8,128)(2,1)} %bitcast.28, f32[8,1,4,2]{0,2,1,3:T(4,128)S(1)} %get-tuple-element.21, f32[8,1,4,2]{0,2,1,3:T(4,128)S(1)} %get-tuple-element.20), kind=kOutput, calls=%fused_computation.18 | convolution fusion | flops 67109504 | bytes 16777728 | tf_op jit(solution)/shard_map/wgpfci,pcbd->bwgfdi/dot_general | solution.py:98
  208.9 16.7 %fusion.7 = bf16[4,2,128,8,256]{4,0,3,2,1:T(4,128)(2,1)} fusion(f32[4,2,128,8,256,1]{4,0,5,3,2,1:T(4,128)} %fusion.8, bf16[8,128,1,8,2,256]{5,3,4,2,1,0:T(8,128)(2,1)} %bitcast.28, f32[8,1,4,2]{0,2,1,3:T(4,128)S(1)} %get-tuple-element.21, f32[8,1,4,2]{0,2,1,3:T(4,128)S(1)} %get-tuple-element.20), kind=kOutput, calls=%fused_computation.17 | convolution fusion | flops 71303680 | bytes 20972032 | tf_op jit(solution)/shard_map/wgpfci,pcbd->bwgfdi/dot_general | solution.py:96
  225.6 4.3 copy.48
  229.9 0.0 copy-start
  229.9 1.9 copy-done
  231.8 2.8 copy.54
  234.6 0.0 all-gather.2.cloned.1.call-update
  234.6 7.5 %copy.51 = bf16[4,8,1,256,256]{3,4,2,1,0:T(8,128)(2,1)} copy(bf16[4,8,1,256,256]{4,0,3,1,2:T(4,128)(2,1)} %bitcast.94) | data formatting | bytes 8388608 | tf_op jit(solution)/shard_map/stack;reshape;reshape | solution.py:107
  242.1 3.8 fusion.58
  245.9 1.2 copy.68
  247.1 2.4 copy_negate_fusion
  249.5 2.3 pad_maximum_fusion
  251.8 7.6 %copy.52 = bf16[4,8,1,256,256]{3,4,2,1,0:T(8,128)(2,1)} copy(bf16[4,8,1,256,256]{4,1,3,0,2:T(8,128)(2,1)} %bitcast.97) | data formatting | bytes 8388608 | tf_op jit(solution)/shard_map/stack;reshape | solution.py:107
  259.4 261.7 %all-gather.2.cloned.1.call-done = bf16[4,8,256,1024]{3,2,1,0:T(8,128)(2,1)} async-done(((bf16[4,8,256,256]{3,2,1,0:T(8,128)(2,1)}), bf16[4,8,256,1024]{3,2,1,0:T(8,128)(2,1)}) %all-gather.2.cloned.1.call-update) | async-done | bytes 16777232 | tf_op jit(solution)/shard_map/all_gather | solution.py:115
  521.2 31.3 %convolution_multiply_fusion = f32[4,8,2,256,1024]{4,3,2,1,0:T(8,128)} fusion(bf16[4,8,256,1024]{3,2,1,0:T(8,128)(2,1)} %all-gather.2.cloned.1.call-done, bf16[4,8,1,256,256]{3,4,2,1,0:T(8,128)(2,1)} %copy.52, bf16[4,8,1,256,256]{3,4,2,1,0:T(8,128)(2,1)} %copy.51), kind=kOutput, calls=%fused_computation | convolution fusion | flops 8610906112 | bytes 92274688 | tf_op jit(solution)/shard_map/bsokn,bskw->bsonw/dot_general | solution.py:112
  (5 shorter events, 0.0 us)
Async XLA Ops:
  85.5 110.8 %all-to-all-start = ((bf16[1024,1,8,2,256]{4,2,3,1,0:T(8,128)(2,1)}), bf16[1024,1,8,2,256]{4,2,3,1,0:T(8,128)(2,1)}, u32[]{:S(2)}, u32[]{:S(2)}) async-start(bf16[1024,1,8,2,256]{4,2,3,1,0:T(8,128)(2,1)} %bitcast.95), calls=%async_computation | async-start | bytes 16777216 | tf_op jit(solution)/shard_map/all_to_all | solution.py:90
  101.5 419.6 %all-gather.2.cloned.1.call-start = ((), (), s32[]{:S(2)}) async-start(), calls=%async_computation.1 | async-start | bytes 20971520 | tf_op jit(solution)/shard_map/all_gather | solution.py:115
  229.9 2.0 copy-start
Sparse Core Ops, SparseCore 0:
  234.8 286.3 all-gather.1
where the time goes:
time: 566 us; the launch traced here: 560 us
  waiting for transfers between devices  356 us (63%)
  matrix products  99.8 us (18%)
  local copies, waits for them, and re-layouts  55.6 us (10%)
  other arithmetic  18 us (3%)
  starting transfers between devices  16 us (3%)
  between operations  13.7 us (2%)
    all_gather x1, waiting for transfers between devices, per_device(): lax.all_gather(columns, 'stn', axis=3, tiled=True)  262 us
    all_to_all x1, waiting for transfers between devices, per_device(): lax.all_to_all(branch, 'chan', split_axis=0, concat_axis=1, tiled=True)  94.6 us
    dot_general x1, matrix products, per_device(): jnp.einsum(vis_form, left_side, lax.all_gather(columns, 'stn', axis=3, ti...  31.3 us
    dot_general x1, matrix products, per_device(): jnp.einsum('rvcfi,ruvcd->uvfdi', inner, twist_table, precision=better, pr...  25 us
    dot_general x1, matrix products, per_device(): jnp.einsum(phase_form, grouped, band_upper, preferred_element_type=jnp.fl...  16.7 us
    all_to_all x1, starting transfers between devices, per_device(): lax.all_to_all(branch, 'chan', split_axis=0, concat_axis=1, tiled=True)  16 us
    another operation x2, local copies, waits for them, and re-layouts, per_device(): left_side = jnp.stack([columns, swapped], axis=2)  15 us
    dot_general x1, matrix products, per_device(): jnp.einsum('ifqr,qvc->rvcfi', folded, short_table, precision=better, pref...  14.2 us
  transfers between devices with their start and end apart: 2, of which 2 were waited for; matrix products, arithmetic and copies ran while one was open for 4% of the time, Pallas kernels for 0%

commit v1 on v0

--- a/solution.py
+++ b/solution.py
@@ -1,3 +1,4 @@
+import functools
 import math
 import jax
 import jax.numpy as jnp
@@ -5,6 +6,19 @@
 from jax.sharding import PartitionSpec as P
 
 AVG = 16
+
+
+def roots_store(mat, row_axis):
+    f_now = jnp.concatenate(
+        lax.all_to_all(
+            jnp.stack(jnp.split(mat, lax.axis_size(row_axis), axis=0), axis=0), row_axis, 0, 0
+        ),
+        axis=1,
+    )
+    return f_now
+
+
+part_ranges_by_axis = functools.partial(roots_store, row_axis="chan")
 
 
 def shifted(block, axis, distance):
@@ -87,7 +101,7 @@
     )
     band_table = complex_table(band_re, band_im, 1)
     band_upper, band_lower = split_pair(band_table)
-    turned = lax.all_to_all(branch, "chan", split_axis=0, concat_axis=1, tiled=True)
+    turned = part_ranges_by_axis(branch)
     span_len = turned.shape[0]
     sources = turned.shape[1]
     item_count = turned.shape[2]

time: 566 us -> 601 us (1.062)
  local copies, waits for them, and re-layouts: 55.6 us -> 101 us
  starting transfers between devices: 16 us -> 5.45 us
    split x0 -> x1, local copies, waits for them, and re-layouts: none -> 39.5 us  [roots_store(): jnp.split(mat, lax.axis_size(row_axis), axis=0)]
    all_to_all x1, starting transfers between devices: 16 us -> 5.2 us  [roots_store(): lax.all_to_all(jnp.stack(jnp.split(mat, lax.axis_size(row_axis), axis=0),...]
    convert_element_type x1 -> x0, local copies, waits for them, and re-layouts: 8.52 us -> none  [per_device(): branch.reshape(slot_count, 1, frames_dev, 2, inputs_dev)]
    another operation x0 -> x2, local copies, waits for them, and re-layouts: none -> 7.86 us  [roots_store(): jnp.stack(jnp.split(mat, lax.axis_size(row_axis), axis=0), axis=0)]
    unnamed x4 -> x13, local copies, waits for them, and re-layouts: 10 us -> 16.9 us
where the time goes in v1:
time: 601 us; the launch traced here: 595 us
  waiting for transfers between devices  356 us (59%)
  local copies, waits for them, and re-layouts  101 us (17%)
  matrix products  100 us (17%)
  other arithmetic  17.7 us (3%)
  between operations  14.1 us (2%)
    all_gather x1, waiting for transfers between devices, per_device(): lax.all_gather(columns, 'stn', axis=3, tiled=True)  262 us
    all_to_all x1, waiting for transfers between devices, roots_store(): lax.all_to_all(jnp.stack(jnp.split(mat, lax.axis_size(row_axis), axis=0),...  94.2 us
    split x1, local copies, waits for them, and re-layouts, roots_store(): jnp.split(mat, lax.axis_size(row_axis), axis=0)  39.5 us
    dot_general x1, matrix products, per_device(): jnp.einsum(vis_form, left_side, lax.all_gather(columns, 'stn', axis=3, ti...  31.3 us
    dot_general x1, matrix products, per_device(): jnp.einsum('rvcfi,ruvcd->uvfdi', inner, twist_table, precision=better, pr...  25.1 us
    dot_general x1, matrix products, per_device(): jnp.einsum(phase_form, grouped, band_upper, preferred_element_type=jnp.fl...  17 us
    unnamed x13, local copies, waits for them, and re-layouts  16.9 us
    another operation x2, local copies, waits for them, and re-layouts, per_device(): left_side = jnp.stack([columns, swapped], axis=2)  15 us
  transfers between devices with their start and end apart: 2, of which 2 were waited for; matrix products, arithmetic and copies ran while one was open for 4% of the time, Pallas kernels for 0%

profile of v1, /device:TPU:0, one launch (start us, length us, event | category | flops | bytes accessed | tf_op | source)
XLA Modules:
  0.0 594.6 jit_solution(12672252521858460353)
XLA Ops:
  7.1 0.5 copy.208
  7.6 0.5 copy.209
  8.1 6.8 %copy.210 = bf16[256,1,8,1024]{0,3,2,1:T(8,128)(2,1)} copy(bf16[256,1,8,1024]{3,2,1,0:T(8,128)(2,1)} %param.2) | data formatting | bytes 8388608 | tf_op args[0]
  15.0 1.1 constant_dynamic-slice_fusion.6
  16.0 12.3 %multiply_bitcast_fusion = f32[256,8,128,8]{0,3,2,1:T(8,128)} fusion(bf16[256,8,1024]{0,2,1:T(8,128)(2,1)} %bitcast.109, f32[8]{0:T(128)S(1)} %compare_convert_fusion, f32[1024]{0:T(1024)S(1)} %bitcast.120, f32[1024]{0:T(1024)S(1)} %bitcast.114, f32[1024]{0:T(1024)S(1)} %bitcast.115, f32[1024]{0:T(1024)S(1)} %bitcast.116, f32[1024]{0:T(1024)S(1)} %bitcast.117, ...), kind=kLoop, calls=%fused_computation.24 | loop fusion | flops 50331648 | bytes 12615712 | tf_op jit(solution)/shard_map/reshape | solution.py:77
  28.4 9.2 %copy.211 = f32[256,8,128,8]{2,0,3,1:T(8,128)} copy(f32[256,8,128,8]{0,3,2,1:T(8,128)} %multiply_bitcast_fusion) | data formatting | bytes 16777216 | tf_op jit(solution)/shard_map/reshape | solution.py:77
  37.5 14.1 %fusion.18 = f32[8,128,2,8,256,1]{4,1,0,3,2,5:T(8,128)} fusion(f32[256,8,128,8]{2,0,3,1:T(8,128)} %copy.211, f32[128,128,1]{0,1,2:T(8,128)S(1)} %get-tuple-element.32, f32[128,128,1]{0,1,2:T(8,128)S(1)} %get-tuple-element.33), kind=kOutput, calls=%fused_computation.27 | convolution fusion | flops 3221258240 | bytes 25296896 | tf_op jit(solution)/shard_map/ifqr,qvc->rvcfi/dot_general | solution.py:81
  51.6 25.1 %fusion.3 = bf16[8,128,8,2,256]{4,0,2,3,1:T(8,128)(2,1)} fusion(f32[8,128,2,8,256,1]{4,1,0,3,2,5:T(8,128)} %fusion.18, f32[8,8,128,1,2]{0,1,3,4,2:T(8,128)S(1)} %bitcast.112, f32[8,8,128,1,2]{0,1,3,4,2:T(8,128)S(1)} %bitcast.111), kind=kOutput, calls=%fused_computation.12 | convolution fusion | flops 406880256 | bytes 25296896 | tf_op jit(solution)/shard_map/rvcfi,ruvcd->uvfdi/dot_general | solution.py:90
  76.7 39.5 %fusion.58 = (bf16[1,128,8,2,256]{4,0,2,3,1:T(2,128)(2,1)S(1)}, bf16[1,128,8,2,256]{4,0,2,3,1:T(2,128)(2,1)S(1)}, bf16[1,128,8,2,256]{4,0,2,3,1:T(2,128)(2,1)S(1...) fusion(bf16[8,128,8,2,256]{4,0,2,3,1:T(8,128)(2,1)} %fusion.3), kind=kLoop, calls=%fused_computation.100 | loop fusion | bytes 16777216 | tf_op jit(solution)/shard_map/split | solution.py:14
  116.2 2.0 bitcast_dynamic-update-slice_fusion.7
  118.3 1.9 bitcast_dynamic-update-slice_fusion.6
  120.1 1.9 bitcast_dynamic-update-slice_fusion.5
  122.3 0.3 bitcast_dynamic-update-slice_fusion.3
  122.6 0.3 bitcast_dynamic-update-slice_fusion.2
  122.9 0.3 bitcast_dynamic-update-slice_fusion.1
  123.2 0.3 bitcast_dynamic-update-slice_fusion
  123.5 7.6 %copy.213 = bf16[8,128,1,8,2,256]{5,4,3,1,2,0:T(2,128)(2,1)} copy(bf16[8,128,1,8,2,256]{5,3,4,2,1,0:T(8,128)(2,1)S(1)} %bitcast_dynamic-update-slice_fusion) | data formatting | bytes 16777216 | tf_op jit(solution)/shard_map/stack | solution.py:14
  131.1 5.2 all-to-all-start
  136.7 94.2 %all-to-all-done = bf16[8,128,1,8,2,256]{5,4,3,1,2,0:T(2,128)(2,1)} async-done(((bf16[8,128,1,8,2,256]{5,4,3,1,2,0:T(2,128)(2,1)}), bf16[8,128,1,8,2,256]{5,4,3,1,2,0:T(2,128)(2,1)}, u32[]{:S(2)}, u32[]{:S(2)}) %all-to-all-start) | async-done | bytes 8388640 | tf_op jit(solution)/shard_map/all_to_all | solution.py:13
  230.8 12.5 %fusion.8 = f32[4,2,128,8,256,1]{4,0,5,3,2,1:T(4,128)} fusion(bf16[8,128,1,8,2,256]{5,4,3,1,2,0:T(2,128)(2,1)} %all-to-all-done, f32[8,1,4,2]{0,2,1,3:T(4,128)S(1)} %get-tuple-element.29, f32[8,1,4,2]{0,2,1,3:T(4,128)S(1)} %get-tuple-element.28), kind=kOutput, calls=%fused_computation.18 | convolution fusion | flops 67109504 | bytes 16777728 | tf_op jit(solution)/shard_map/wgpfci,pcbd->bwgfdi/dot_general | solution.py:112
  243.4 17.0 %fusion.7 = bf16[4,2,128,8,256]{4,0,3,2,1:T(4,128)(2,1)} fusion(f32[4,2,128,8,256,1]{4,0,5,3,2,1:T(4,128)} %fusion.8, bf16[8,128,1,8,2,256]{5,4,3,1,2,0:T(2,128)(2,1)} %all-to-all-done, f32[8,1,4,2]{0,2,1,3:T(4,128)S(1)} %get-tuple-element.29, f32[8,1,4,2]{0,2,1,3:T(4,128)S(1)} %get-tuple-element.28), kind=kOutput, calls=%fused_computation.17 | convolution fusion | flops 71303680 | bytes 20972032 | tf_op jit(solution)/shard_map/wgpfci,pcbd->bwgfdi/dot_general | solution.py:110
  260.4 4.3 copy.215
  264.7 2.0 copy-done
  266.7 2.8 copy.221
  269.4 7.5 %copy.218 = bf16[4,8,1,256,256]{3,4,2,1,0:T(8,128)(2,1)} copy(bf16[4,8,1,256,256]{4,0,3,1,2:T(4,128)(2,1)} %bitcast.108) | data formatting | bytes 8388608 | tf_op jit(solution)/shard_map/stack;reshape;reshape | solution.py:121
  276.9 3.9 fusion.59
  280.8 1.2 copy.241
  282.0 2.4 copy_negate_fusion
  284.4 2.3 pad_maximum_fusion
  286.8 7.5 %copy.219 = bf16[4,8,1,256,256]{3,4,2,1,0:T(8,128)(2,1)} copy(bf16[4,8,1,256,256]{4,1,3,0,2:T(8,128)(2,1)} %bitcast.110) | data formatting | bytes 8388608 | tf_op jit(solution)/shard_map/stack;reshape | solution.py:121
  294.3 261.7 %all-gather.2.cloned.1.call-done = bf16[4,8,256,1024]{3,2,1,0:T(8,128)(2,1)} async-done(((bf16[4,8,256,256]{3,2,1,0:T(8,128)(2,1)}), bf16[4,8,256,1024]{3,2,1,0:T(8,128)(2,1)}) %all-gather.2.cloned.1.call-update) | async-done | bytes 16777232 | tf_op jit(solution)/shard_map/all_gather | solution.py:129
  556.0 31.3 %convolution_multiply_fusion = f32[4,8,2,256,1024]{4,3,2,1,0:T(8,128)} fusion(bf16[4,8,256,1024]{3,2,1,0:T(8,128)(2,1)} %all-gather.2.cloned.1.call-done, bf16[4,8,1,256,256]{3,4,2,1,0:T(8,128)(2,1)} %copy.219, bf16[4,8,1,256,256]{3,4,2,1,0:T(8,128)(2,1)} %copy.218), kind=kOutput, calls=%fused_computation | convolution fusion | flops 8610906112 | bytes 92274688 | tf_op jit(solution)/shard_map/bsokn,bskw->bsonw/dot_general | solution.py:126
  (15 shorter events, 1.2 us)
Async XLA Ops:
  116.2 5.8 copy-start.1
  131.1 99.7 %all-to-all-start = ((bf16[8,128,1,8,2,256]{5,4,3,1,2,0:T(2,128)(2,1)}), bf16[8,128,1,8,2,256]{5,4,3,1,2,0:T(2,128)(2,1)}, u32[]{:S(2)}, u32[]{:S(2)}) async-start(bf16[8,128,1,8,2,256]{5,4,3,1,2,0:T(2,128)(2,1)} %copy.213), calls=%async_computation | async-start | bytes 16777216 | tf_op jit(solution)/shard_map/all_to_all | solution.py:13
  136.3 419.7 %all-gather.2.cloned.1.call-start = ((), (), s32[]{:S(2)}) async-start(), calls=%async_computation.1 | async-start | bytes 20971520 | tf_op jit(solution)/shard_map/all_gather | solution.py:129
  264.7 2.0 copy-start
Sparse Core Ops, SparseCore 0:
  269.6 286.3 all-gather.1
